TPU v7x, 256 devices: a whole 4x4x8 slice. The times are simulated.
256 devices in a mesh: layer: 4 (over y_hi, core), feat: 64 (over y_lo, z, x).
Axes of the slice: x: 4, y: 4 (y_hi: 2, y_lo: 2; y = y_hi * 2 + y_lo), z: 8, core: 2. Of those that a mesh axis runs over, the one named last changes fastest.
Arguments:
- inputs: bfloat16 [768, 4, 2048], P('feat', 'layer'), may hold values from -6 to 6
- w_enc: bfloat16 [4, 2048, 16384], P('layer', None, 'feat'), may hold values from -6 to 6
- b_enc: bfloat16 [16384], P('feat'), may hold values from -3 to 3
- w_dec: bfloat16 [16384, 4, 2048], P('feat', 'layer'), may hold values from -15 to 15
- b_dec: bfloat16 [4, 2048], P('layer'), may hold values from -3 to 3
Outputs:
- recon: bfloat16 [768, 4, 2048], P('feat', 'layer')
- new_enc: float32 [4, 2048, 16384], P('layer', None, 'feat')
- new_dec: float32 [16384, 4, 2048], P('feat', 'layer')
All inputs are finite; a program needn't handle non-finite values.
Results may differ from a plain program's by a relative error of at most 0.0055.
Values may be sent and summed in bfloat16 or wider, within the bound.
No kernel may reach another device: no remote copies, remote signals or barrier semaphores. Data moves between devices by JAX's collectives and lax.ppermute only.
A program may use at most 64 MiB of HBM per device.

v0:
```python
import math
import jax
import jax.numpy as jnp
from jax import lax
from jax.sharding import PartitionSpec as P

D = 2048
F = 16384
L = 4
LEARN_RATE = 1.0
SHRINK_LEVEL = 0.5
EPSILON = 1e-06


def body(inputs, w_enc, b_enc, w_dec, b_dec):
    token_rows, layer_count, model_width = inputs.shape
    feature_count = w_enc.shape[2]
    flat_width = layer_count * model_width
    scale_enc = 1.0 / math.sqrt(L * D)
    scale_dec = 1.0 / math.sqrt(F)
    x_local = inputs.reshape(token_rows, flat_width)
    x_all = lax.all_gather(x_local, "feat", axis=0, tiled=True)
    enc_mat = w_enc.reshape(flat_width, feature_count)
    dec_mat = w_dec.reshape(feature_count, flat_width)
    pre_part = jnp.dot(x_all, enc_mat, preferred_element_type=jnp.float32)
    pre_act = lax.psum(pre_part, "layer") * scale_enc + b_enc.astype(jnp.float32)
    latent = jnp.maximum(pre_act, 0.0).astype(jnp.bfloat16)
    bias_flat = b_dec.reshape(flat_width).astype(jnp.float32)
    summed = lax.psum_scatter(
        jnp.dot(latent, dec_mat, preferred_element_type=jnp.float32),
        "feat",
        scatter_dimension=0,
        tiled=True,
    )
    recon_local = summed * scale_dec + bias_flat
    err_local = (recon_local - x_local.astype(jnp.float32)).astype(jnp.bfloat16)
    err_all = lax.all_gather(err_local, "feat", axis=0, tiled=True)
    recon = recon_local.astype(jnp.bfloat16).reshape(token_rows, layer_count, model_width)
    grad_part = lax.dot_general(
        err_all, dec_mat, (((1,), (1,)), ((), ())), preferred_element_type=jnp.float32
    )
    grad_dec = (
        lax.dot_general(
            latent, err_all, (((0,), (0,)), ((), ())), preferred_element_type=jnp.float32
        )
        * scale_dec
    )
    half_dec = dec_mat.astype(jnp.float32) - LEARN_RATE * grad_dec
    square_part = jnp.sum(half_dec * half_dec, axis=1)
    grad_sum, square_sum = (
        lax.psum(grad_part.astype(jnp.bfloat16), "layer").astype(jnp.float32),
        lax.psum(square_part.astype(jnp.bfloat16), "layer").astype(jnp.float32),
    )
    grad_latent = grad_sum * scale_dec
    grad_pre = jnp.where(pre_act > 0.0, grad_latent, 0.0).astype(jnp.bfloat16)
    grad_enc = (
        lax.dot_general(
            x_all, grad_pre, (((0,), (0,)), ((), ())), preferred_element_type=jnp.float32
        )
        * scale_enc
    )
    new_enc = (enc_mat.astype(jnp.float32) - LEARN_RATE * grad_enc).reshape(
        layer_count, model_width, feature_count
    )
    row_rms = jnp.sqrt(square_sum / (L * D) + EPSILON)
    factor = jnp.maximum(0.0, 1.0 - SHRINK_LEVEL / row_rms)
    new_dec = (half_dec * factor[:, None]).reshape(feature_count, layer_count, model_width)
    return (recon, new_enc, new_dec)


def solution(mesh):
    return jax.shard_map(
        body,
        mesh=mesh,
        in_specs=(
            P("feat", "layer", None),
            P("layer", None, "feat"),
            P("feat"),
            P("feat", "layer", None),
            P("layer", None),
        ),
        out_specs=(P("feat", "layer", None), P("layer", None, "feat"), P("feat", "layer", None)),
        check_vma=False,
    )
```

profile of v0, /device:TPU:1, one launch (start us, length us, event | category | flops | bytes accessed | tf_op | source)
XLA Modules:
  0.0 1049.1 jit_solution(5644969104625668437)
XLA Ops:
  7.2 0.0 all-gather.5.cloned.1.call-start
  7.2 1.6 copy.18
  8.8 0.0 all-gather.5.cloned.1.call-update
  8.8 0.0 all-reduce.5.cloned.1.call-start
  8.9 267.4 %all-gather.5.cloned.1.call-done = bf16[768,1,2048]{2,1,0:T(2,128)(2,1)} async-done(((bf16[12,1,2048]{2,1,0:T(2,128)(2,1)}), bf16[768,1,2048]{2,1,0:T(2,128)(2,1)}) %all-gather.5.cloned.1.call-update) | async-done | bytes 3145744 | tf_op jit(solution)/shard_map/all_gather | solution.py:22
  276.2 5.8 fusion.3
  282.0 0.0 all-reduce.5.cloned.1.call-update
  282.0 0.0 all-gather.7.cloned.1.call-start
  282.1 91.4 %all-reduce.5.cloned.1.call-done = f32[768,256]{1,0:T(8,128)} async-done(((f32[768,256]{1,0:T(8,128)}), f32[768,256]{1,0:T(8,128)}) %all-reduce.5.cloned.1.call-update) | async-done | bytes 786448 | tf_op jit(solution)/shard_map/psum | solution.py:26
  373.5 4.7 fusion.22
  378.2 162.5 %fusion = f32[16,2048]{1,0:T(8,128)S(1)} fusion(f32[768,2048]{1,0:T(8,128)} %fusion.22), kind=kCustom, calls=%all-reduce-scatter | all-reduce-scatter fusion | flops 2097153 | bytes 6423552
  540.8 0.0 copy-start.4
  540.8 1.4 collective-permute-start.15
  542.3 1.3 collective-permute-start
  543.6 1.3 collective-permute-start.1
  544.9 6.4 collective-permute-start.10
  551.3 3.7 collective-permute-start.11
  555.1 7.0 collective-permute-start.12
  562.2 1.6 collective-permute-start.13
  563.8 4.3 collective-permute-start.14
  568.2 5.8 collective-permute-start.2
  574.0 1.3 collective-permute-start.3
  575.3 4.1 collective-permute-start.4
  579.4 3.3 collective-permute-start.5
  582.8 8.8 collective-permute-start.6
  591.6 3.1 collective-permute-start.7
  594.7 4.4 collective-permute-start.8
  599.2 2.6 collective-permute-start.9
  601.9 0.6 dynamic-slice.4
  603.2 1.0 collective-permute-done.8
  604.2 0.6 copy-done.19
  604.8 7.7 collective-permute-done.9
  612.5 16.4 %concatenate = f32[268,2048]{1,0:T(8,128)S(1)} concatenate(f32[12,2048]{1,0:T(8,128)} %copy-done.5, f32[16,2048]{1,0:T(8,128)} %copy-done.12, f32[16,2048]{1,0:T(8,128)} %copy-done.11, f32[16,2048]{1,0:T(8,128)} %copy-done.10, f32[16,2048]{1,0:T(8,128)} %copy-done.9, f32[16,2048]{1,0:T(8,128)} %copy-done.8, f32[16,2048]{1,0:T(8,128)} %collective-permute-done.9, ...), dimensions={0} | concatenate | bytes 4390912
  628.9 0.7 fusion.32
  629.6 0.0 all-gather.7.cloned.1.call-update
  629.6 0.0 all-reduce.7.cloned.1.call-start
  629.7 1.4 copy.19
  631.1 292.3 %all-gather.7.cloned.1.call-done = bf16[64,12,2048]{2,1,0:T(8,128)(2,1)} async-done(((bf16[1,12,2048]{2,1,0:T(8,128)(2,1)}), bf16[64,12,2048]{2,1,0:T(8,128)(2,1)}) %all-gather.7.cloned.1.call-update) | async-done | bytes 3145744 | tf_op jit(solution)/shard_map/all_gather | solution.py:37
  923.5 6.2 reshape.37
  929.6 3.7 convolution_convert_fusion
  933.4 3.3 multiply_reduce_fusion
  936.7 53.0 %psum.23 = bf16[256]{0:T(256)(128)(2,1)S(1)} all-reduce(bf16[256]{0:T(256)(128)(2,1)S(1)} %get-tuple-element.17), channel_id=1, replica_groups=mesh['layer'=4,'feat'=64] {'layer'}, use_global_device_ids=true, to_apply=%region_4.0 | all-reduce | flops 256 | bytes 1024 | tf_op jit(solution)/shard_map/psum | solution.py:52
  989.8 0.0 all-reduce.7.cloned.1.call-update
  989.8 0.2 multiply_bitcast_fusion
  990.0 3.5 copy.21
  993.5 41.8 %all-reduce.7.cloned.1.call-done = bf16[768,256]{1,0:T(8,128)(2,1)} async-done(((bf16[768,256]{1,0:T(8,128)(2,1)}), bf16[768,256]{1,0:T(8,128)(2,1)}) %all-reduce.7.cloned.1.call-update) | async-done | bytes 393232 | tf_op jit(solution)/shard_map/psum | solution.py:51
  1035.3 5.5 fusion.14
  1040.8 1.8 copy.20
  (62 shorter events, 0.2 us)
Async XLA Ops:
  7.2 269.1 %all-gather.5.cloned.1.call-start = ((), (), s32[]{:S(2)}) async-start(), calls=%async_computation.2 | async-start | bytes 6389760 | tf_op jit(solution)/shard_map/all_gather | solution.py:22
  8.8 273.3 %copy-start.22 = (bf16[256]{0:T(256)(128)(2,1)S(1)}, bf16[256]{0:T(256)(128)(2,1)}, u32[]{:S(2)}) copy-start(bf16[256]{0:T(256)(128)(2,1)} %param.7) | copy-start | bytes 1540
  8.8 364.7 %copy-start.2 = (bf16[256,1,2048]{2,0,1:T(8,128)(2,1)S(1)}, bf16[256,1,2048]{2,0,1:T(8,128)(2,1)}, u32[]{:S(2)}) copy-start(bf16[256,1,2048]{2,0,1:T(8,128)(2,1)} %param.8) | copy-start | bytes 3145732
  8.8 364.7 %all-reduce.5.cloned.1.call-start = ((), (), s32[]{:S(2)}) async-start(), calls=%async_computation | async-start | bytes 1572864 | tf_op jit(solution)/shard_map/psum | solution.py:26
  282.0 641.4 %all-gather.7.cloned.1.call-start = ((), (), s32[]{:S(2)}) async-start(), calls=%async_computation.3 | async-start | bytes 4259840 | tf_op jit(solution)/shard_map/all_gather | solution.py:37
  378.2 223.6 %copy-start.20 = (bf16[1,2048]{1,0:T(2,128)(2,1)S(1)}, bf16[1,2048]{1,0:T(2,128)(2,1)}, u32[]{:S(2)}) copy-start(bf16[1,2048]{1,0:T(2,128)(2,1)} %param.9) | copy-start | bytes 12292
  378.2 223.6 %copy-start.21 = (u32[256]{0:T(256)S(1)}, u32[256]{0:T(256)}, u32[]{:S(2)}) copy-start(u32[256]{0:T(256)} %constant.26) | copy-start | bytes 3076
  540.8 88.1 %copy-start.4 = (bf16[12,1,2048]{2,0,1:T(8,128)(2,1)S(1)}, bf16[12,1,2048]{2,0,1:T(8,128)(2,1)}, u32[]{:S(2)}) copy-start(bf16[12,1,2048]{2,0,1:T(8,128)(2,1)} %param.5) | copy-start | bytes 147460
  540.8 88.9 %copy-start.1 = (bf16[1,2048,256]{2,1,0:T(8,128)(2,1)S(1)}, bf16[1,2048,256]{2,1,0:T(8,128)(2,1)}, u32[]{:S(2)}) copy-start(bf16[1,2048,256]{2,1,0:T(8,128)(2,1)} %param.6) | copy-start | bytes 3145732
  540.8 14.2 %collective-permute-start.15 = (f32[12,2048]{1,0:T(8,128)S(1)}, f32[12,2048]{1,0:T(8,128)S(1)}, u32[]{:S(2)}, u32[]{:S(2)}) collective-permute-start(f32[12,2048]{1,0:T(8,128)S(1)} %slice), channel_id=1, source_target_pairs={{0,16},{1,17},{2,18},{3,19},{4,20},{5,21},{6,22},{7,23},{8,24},{9,... | collective-permute-start | bytes 294920
  542.3 19.9 %collective-permute-start = (f32[16,2048]{1,0:T(8,128)S(1)}, f32[16,2048]{1,0:T(8,128)S(1)}, u32[]{:S(2)}, u32[]{:S(2)}) collective-permute-start(f32[16,2048]{1,0:T(8,128)S(1)} %fusion), channel_id=1, source_target_pairs={{0,1},{1,2},{2,3},{3,4},{4,5},{5,6},{6,7},{7,8},{8,9},{9,10},{10,1... | collective-permute-start | bytes 393224
  543.6 20.2 %collective-permute-start.1 = (f32[16,2048]{1,0:T(8,128)S(1)}, f32[16,2048]{1,0:T(8,128)S(1)}, u32[]{:S(2)}, u32[]{:S(2)}) collective-permute-start(f32[16,2048]{1,0:T(8,128)S(1)} %fusion), channel_id=1, source_target_pairs={{0,2},{1,3},{2,4},{3,5},{4,6},{5,7},{6,8},{7,9},{8,10},{9,11},{10,... | collective-permute-start | bytes 393224
  544.9 23.3 %collective-permute-start.10 = (f32[16,2048]{1,0:T(8,128)S(1)}, f32[16,2048]{1,0:T(8,128)S(1)}, u32[]{:S(2)}, u32[]{:S(2)}) collective-permute-start(f32[16,2048]{1,0:T(8,128)S(1)} %fusion), channel_id=1, source_target_pairs={{0,11},{1,12},{2,13},{3,14},{4,15},{5,16},{6,17},{7,18},{8,19},{9,... | collective-permute-start | bytes 393224
  551.3 22.6 %collective-permute-start.11 = (f32[16,2048]{1,0:T(8,128)S(1)}, f32[16,2048]{1,0:T(8,128)S(1)}, u32[]{:S(2)}, u32[]{:S(2)}) collective-permute-start(f32[16,2048]{1,0:T(8,128)S(1)} %fusion), channel_id=1, source_target_pairs={{0,12},{1,13},{2,14},{3,15},{4,16},{5,17},{6,18},{7,19},{8,20},{9,... | collective-permute-start | bytes 393224
  555.1 44.0 %copy-start.5 = (f32[12,2048]{1,0:T(8,128)}, f32[12,2048]{1,0:T(8,128)S(1)}, u32[]{:S(2)}) copy-start(f32[12,2048]{1,0:T(8,128)S(1)} %collective-permute-done.15) | copy-start | bytes 294916
  555.1 20.2 %collective-permute-start.12 = (f32[16,2048]{1,0:T(8,128)S(1)}, f32[16,2048]{1,0:T(8,128)S(1)}, u32[]{:S(2)}, u32[]{:S(2)}) collective-permute-start(f32[16,2048]{1,0:T(8,128)S(1)} %fusion), channel_id=1, source_target_pairs={{0,13},{1,14},{2,15},{3,16},{4,17},{5,18},{6,19},{7,20},{8,21},{9,... | collective-permute-start | bytes 393224
  562.1 39.6 %copy-start.6 = (f32[16,2048]{1,0:T(8,128)}, f32[16,2048]{1,0:T(8,128)S(1)}, u32[]{:S(2)}) copy-start(f32[16,2048]{1,0:T(8,128)S(1)} %collective-permute-done) | copy-start | bytes 393220
  562.2 17.3 %collective-permute-start.13 = (f32[16,2048]{1,0:T(8,128)S(1)}, f32[16,2048]{1,0:T(8,128)S(1)}, u32[]{:S(2)}, u32[]{:S(2)}) collective-permute-start(f32[16,2048]{1,0:T(8,128)S(1)} %fusion), channel_id=1, source_target_pairs={{0,14},{1,15},{2,16},{3,17},{4,18},{5,19},{6,20},{7,21},{8,22},{9,... | collective-permute-start | bytes 393224
  563.8 37.9 %copy-start.7 = (f32[16,2048]{1,0:T(8,128)}, f32[16,2048]{1,0:T(8,128)S(1)}, u32[]{:S(2)}) copy-start(f32[16,2048]{1,0:T(8,128)S(1)} %collective-permute-done.1) | copy-start | bytes 393220
  563.8 18.9 %collective-permute-start.14 = (f32[16,2048]{1,0:T(8,128)S(1)}, f32[16,2048]{1,0:T(8,128)S(1)}, u32[]{:S(2)}, u32[]{:S(2)}) collective-permute-start(f32[16,2048]{1,0:T(8,128)S(1)} %fusion), channel_id=1, source_target_pairs={{0,15},{1,16},{2,17},{3,18},{4,19},{5,20},{6,21},{7,22},{8,23},{9,... | collective-permute-start | bytes 393224
  568.2 33.6 %copy-start.8 = (f32[16,2048]{1,0:T(8,128)}, f32[16,2048]{1,0:T(8,128)S(1)}, u32[]{:S(2)}) copy-start(f32[16,2048]{1,0:T(8,128)S(1)} %collective-permute-done.10) | copy-start | bytes 393220
  568.2 23.5 %collective-permute-start.2 = (f32[16,2048]{1,0:T(8,128)S(1)}, f32[16,2048]{1,0:T(8,128)S(1)}, u32[]{:S(2)}, u32[]{:S(2)}) collective-permute-start(f32[16,2048]{1,0:T(8,128)S(1)} %fusion), channel_id=1, source_target_pairs={{0,3},{1,4},{2,5},{3,6},{4,7},{5,8},{6,9},{7,10},{8,11},{9,12},{10... | collective-permute-start | bytes 393224
  574.0 27.8 %copy-start.9 = (f32[16,2048]{1,0:T(8,128)}, f32[16,2048]{1,0:T(8,128)S(1)}, u32[]{:S(2)}) copy-start(f32[16,2048]{1,0:T(8,128)S(1)} %collective-permute-done.11) | copy-start | bytes 393220
  574.0 20.7 %collective-permute-start.3 = (f32[16,2048]{1,0:T(8,128)S(1)}, f32[16,2048]{1,0:T(8,128)S(1)}, u32[]{:S(2)}, u32[]{:S(2)}) collective-permute-start(f32[16,2048]{1,0:T(8,128)S(1)} %fusion), channel_id=1, source_target_pairs={{0,4},{1,5},{2,6},{3,7},{4,8},{5,9},{6,10},{7,11},{8,12},{9,13},{1... | collective-permute-start | bytes 393224
  575.3 26.5 %copy-start.10 = (f32[16,2048]{1,0:T(8,128)}, f32[16,2048]{1,0:T(8,128)S(1)}, u32[]{:S(2)}) copy-start(f32[16,2048]{1,0:T(8,128)S(1)} %collective-permute-done.12) | copy-start | bytes 393220
  575.3 23.8 %collective-permute-start.4 = (f32[16,2048]{1,0:T(8,128)S(1)}, f32[16,2048]{1,0:T(8,128)S(1)}, u32[]{:S(2)}, u32[]{:S(2)}) collective-permute-start(f32[16,2048]{1,0:T(8,128)S(1)} %fusion), channel_id=1, source_target_pairs={{0,5},{1,6},{2,7},{3,8},{4,9},{5,10},{6,11},{7,12},{8,13},{9,14},{... | collective-permute-start | bytes 393224
  579.4 22.4 %copy-start.11 = (f32[16,2048]{1,0:T(8,128)}, f32[16,2048]{1,0:T(8,128)S(1)}, u32[]{:S(2)}) copy-start(f32[16,2048]{1,0:T(8,128)S(1)} %collective-permute-done.13) | copy-start | bytes 393220
  579.4 23.7 %collective-permute-start.5 = (f32[16,2048]{1,0:T(8,128)S(1)}, f32[16,2048]{1,0:T(8,128)S(1)}, u32[]{:S(2)}, u32[]{:S(2)}) collective-permute-start(f32[16,2048]{1,0:T(8,128)S(1)} %fusion), channel_id=1, source_target_pairs={{0,6},{1,7},{2,8},{3,9},{4,10},{5,11},{6,12},{7,13},{8,14},{9,15},... | collective-permute-start | bytes 393224
  582.8 19.0 %copy-start.12 = (f32[16,2048]{1,0:T(8,128)}, f32[16,2048]{1,0:T(8,128)S(1)}, u32[]{:S(2)}) copy-start(f32[16,2048]{1,0:T(8,128)S(1)} %collective-permute-done.14) | copy-start | bytes 393220
  582.8 20.4 %collective-permute-start.6 = (f32[16,2048]{1,0:T(8,128)S(1)}, f32[16,2048]{1,0:T(8,128)S(1)}, u32[]{:S(2)}, u32[]{:S(2)}) collective-permute-start(f32[16,2048]{1,0:T(8,128)S(1)} %fusion), channel_id=1, source_target_pairs={{0,7},{1,8},{2,9},{3,10},{4,11},{5,12},{6,13},{7,14},{8,15},{9,16}... | collective-permute-start | bytes 393224
  591.6 10.2 copy-start.13
  591.6 11.5 %collective-permute-start.7 = (f32[16,2048]{1,0:T(8,128)S(1)}, f32[16,2048]{1,0:T(8,128)S(1)}, u32[]{:S(2)}, u32[]{:S(2)}) collective-permute-start(f32[16,2048]{1,0:T(8,128)S(1)} %fusion), channel_id=1, source_target_pairs={{0,8},{1,9},{2,10},{3,11},{4,12},{5,13},{6,14},{7,15},{8,16},{9,17... | collective-permute-start | bytes 393224
  594.7 7.1 copy-start.14
  594.7 9.4 collective-permute-start.8
  599.1 2.7 copy-start.15
  599.2 13.3 %collective-permute-start.9 = (f32[16,2048]{1,0:T(8,128)S(1)}, f32[16,2048]{1,0:T(8,128)}, u32[]{:S(2)}, u32[]{:S(2)}) collective-permute-start(f32[16,2048]{1,0:T(8,128)S(1)} %fusion), channel_id=1, source_target_pairs={{0,10},{1,11},{2,12},{3,13},{4,14},{5,15},{6,16},{7,17},{8,18},{9,... | collective-permute-start | bytes 393224
  603.1 1.0 copy-start.16
  603.1 1.0 copy-start.17
  603.2 1.0 copy-start.18
  604.2 0.7 copy-start.19
  629.6 405.7 %all-reduce.7.cloned.1.call-start = ((), (), s32[]{:S(2)}) async-start(), calls=%async_computation.1 | async-start | bytes 786432 | tf_op jit(solution)/shard_map/psum | solution.py:51
  631.1 298.5 %copy-start.3 = (bf16[256,1,2048]{2,0,1:T(8,128)(2,1)S(1)}, bf16[256,1,2048]{2,0,1:T(8,128)(2,1)}, u32[]{:S(2)}) copy-start(bf16[256,1,2048]{2,0,1:T(8,128)(2,1)} %param.8) | copy-start | bytes 3145732
  929.6 3.7 copy-start
Sparse Core Ops, SparseCore 0:
  10.3 265.8 all-gather.4
  282.2 91.2 all-reduce.4
  629.7 293.6 all-gather.6
  989.9 45.3 all-reduce.6
where the time goes:
time: 1050 us
  waiting for transfers between devices  702 us (67%)
  blocking collectives  216 us (21%)
  starting transfers between devices  60.7 us (6%)
  local copies, waits for them, and re-layouts  32.2 us (3%)
  matrix products  23.1 us (2%)
  between operations  15 us (1%)
    all_gather x1, waiting for transfers between devices, body(): err_all = lax.all_gather(err_local, 'feat', axis=0, tiled=True)  292 us
    all_gather x1, waiting for transfers between devices, body(): x_all = lax.all_gather(x_local, 'feat', axis=0, tiled=True)  267 us
    unnamed x1, blocking collectives  163 us
    psum x1, waiting for transfers between devices, body(): lax.psum(pre_part, 'layer') * scale_enc + b_enc.astype(jnp.float32)  91.4 us
    unnamed x16, starting transfers between devices  60.6 us
    psum x1, blocking collectives, body(): lax.psum(square_part.astype(jnp.bfloat16), 'layer').astype(jnp.float32)  53 us
    psum x1, waiting for transfers between devices, body(): lax.psum(grad_part.astype(jnp.bfloat16), 'layer').astype(jnp.float32)  41.8 us
    unnamed x54, local copies, waits for them, and re-layouts  32.2 us
  transfers between devices with their start and end apart: 20, of which 6 were waited for; matrix products, arithmetic and copies ran while one was open for 1% of the time, Pallas kernels for 0%

commit v1 on v0

--- a/solution.py
+++ b/solution.py
@@ -19,7 +19,10 @@
     scale_enc = 1.0 / math.sqrt(L * D)
     scale_dec = 1.0 / math.sqrt(F)
     x_local = inputs.reshape(token_rows, flat_width)
-    x_all = lax.all_gather(x_local, "feat", axis=0, tiled=True)
+    size = lax.axis_size("feat")
+    blocks = jnp.stack([x_local for _ in range(size)])
+    blocks = lax.all_to_all(blocks, "feat", split_axis=0, concat_axis=0)
+    x_all = jnp.concatenate(blocks, axis=0)
     enc_mat = w_enc.reshape(flat_width, feature_count)
     dec_mat = w_dec.reshape(feature_count, flat_width)
     pre_part = jnp.dot(x_all, enc_mat, preferred_element_type=jnp.float32)

time: 1050 us -> 865 us (0.82)
  waiting for transfers between devices: 702 us -> 391 us
  blocking collectives: 216 us -> 323 us
  local copies, waits for them, and re-layouts: 32.2 us -> 49 us
    all_gather x1 -> x0, waiting for transfers between devices: 267 us -> none  [body(): x_all = lax.all_gather(x_local, 'feat', axis=0, tiled=True)]
    all_to_all x0 -> x1, blocking collectives: none -> 106 us  [body(): blocks = lax.all_to_all(blocks, 'feat', split_axis=0, concat_axis=0)]
    psum x1, waiting for transfers between devices: 91.4 us -> 49.7 us  [body(): lax.psum(pre_part, 'layer') * scale_enc + b_enc.astype(jnp.float32)]
    unnamed x54 -> x35, local copies, waits for them, and re-layouts: 32.2 us -> 42.9 us
  transfers between devices with their start and end apart: 20 -> 19, of which waited for: 6 -> 5; matrix products, arithmetic and copies ran while one was open for 1% -> 1% of each run, Pallas kernels for 0% -> 0%
where the time goes in v1:
time: 865 us; the launch traced here: 863 us
  waiting for transfers between devices  391 us (45%)
  blocking collectives  323 us (37%)
  starting transfers between devices  61.2 us (7%)
  local copies, waits for them, and re-layouts  49 us (6%)
  matrix products  20.9 us (2%)
  between operations  14.8 us (2%)
    all_gather x1, waiting for transfers between devices, body(): err_all = lax.all_gather(err_local, 'feat', axis=0, tiled=True)  292 us
    unnamed x1, blocking collectives  163 us
    all_to_all x1, blocking collectives, body(): blocks = lax.all_to_all(blocks, 'feat', split_axis=0, concat_axis=0)  106 us
    unnamed x16, starting transfers between devices  61.1 us
    psum x1, blocking collectives, body(): lax.psum(square_part.astype(jnp.bfloat16), 'layer').astype(jnp.float32)  53 us
    psum x1, waiting for transfers between devices, body(): lax.psum(pre_part, 'layer') * scale_enc + b_enc.astype(jnp.float32)  49.7 us
    unnamed x35, local copies, waits for them, and re-layouts  42.9 us
    psum x1, waiting for transfers between devices, body(): lax.psum(grad_part.astype(jnp.bfloat16), 'layer').astype(jnp.float32)  40.2 us
  transfers between devices with their start and end apart: 19, of which 5 were waited for; matrix products, arithmetic and copies ran while one was open for 1% of the time, Pallas kernels for 0%

profile of v1, /device:TPU:1, one launch (start us, length us, event | category | flops | bytes accessed | tf_op | source)
XLA Modules:
  0.0 863.3 jit_solution(12469626403897135807)
XLA Ops:
  7.2 0.0 all-reduce.5.cloned.1.call-start
  7.2 1.4 stack.3
  8.6 106.3 %all_to_all.5 = bf16[64,12,2048]{2,1,0:T(8,128)(2,1)} all-to-all(bf16[64,12,2048]{2,1,0:T(8,128)(2,1)S(1)} %stack.3), channel_id=1, replica_groups=mesh['layer'=4,'feat'=64] {'feat'}, dimensions={0} | all-to-all | bytes 6291456 | tf_op jit(solution)/shard_map/all_to_all | solution.py:24
  114.9 4.7 reshape.30
  119.6 0.0 copy-start.13
  119.6 3.1 fusion.5
  122.7 0.0 all-reduce.5.cloned.1.call-update
  122.7 0.0 all-gather.3.cloned.1.call-start
  122.8 49.7 %all-reduce.5.cloned.1.call-done = f32[768,256]{1,0:T(8,128)} async-done(((f32[768,256]{1,0:T(8,128)}), f32[768,256]{1,0:T(8,128)}) %all-reduce.5.cloned.1.call-update) | async-done | bytes 786448 | tf_op jit(solution)/shard_map/psum | solution.py:29
  172.5 5.1 fusion.8
  177.6 163.3 %fusion = f32[16,2048]{1,0:T(8,128)S(1)} fusion(f32[768,2048]{1,0:T(8,128)} %fusion.8), kind=kCustom, calls=%all-reduce-scatter | all-reduce-scatter fusion | flops 2097153 | bytes 6423552
  340.8 0.0 copy-start
  340.9 1.3 collective-permute-start.15
  342.2 1.3 collective-permute-start
  343.5 1.3 collective-permute-start.1
  344.8 5.8 collective-permute-start.10
  350.6 4.0 collective-permute-start.11
  354.6 7.0 collective-permute-start.12
  361.7 1.6 collective-permute-start.13
  363.3 4.3 collective-permute-start.14
  367.7 6.2 collective-permute-start.2
  373.9 1.3 collective-permute-start.3
  375.2 3.0 collective-permute-start.4
  378.2 0.0 copy-start.6
  378.2 4.5 collective-permute-start.5
  382.8 8.4 collective-permute-start.6
  391.1 3.0 collective-permute-start.7
  394.1 6.2 collective-permute-start.8
  400.3 1.9 collective-permute-start.9
  402.4 0.6 dynamic-slice.4
  403.6 2.5 collective-permute-done.8
  406.1 7.0 collective-permute-done.9
  413.1 27.5 %concatenate = f32[268,2048]{1,0:T(8,128)} concatenate(f32[12,2048]{1,0:T(8,128)S(1)} %collective-permute-done.15, f32[16,2048]{1,0:T(8,128)} %copy-done.7, f32[16,2048]{1,0:T(8,128)} %copy-done.6, f32[16,2048]{1,0:T(8,128)} %copy-done.5, f32[16,2048]{1,0:T(8,128)} %copy-done.4, f32[16,2048]{1,0:T(8,128)} %copy-done.3, f32[16,2048]{1,0:T(8,128)} %collective-permute-done.9, ...), dimensions={0} | concatenate | bytes 4390912
  440.6 1.6 fusion.17
  442.2 0.0 all-gather.3.cloned.1.call-update
  442.2 0.0 all-reduce.7.cloned.1.call-start
  442.3 2.3 copy.14
  444.6 291.9 %all-gather.3.cloned.1.call-done = bf16[64,12,2048]{2,1,0:T(8,128)(2,1)} async-done(((bf16[1,12,2048]{2,1,0:T(8,128)(2,1)}), bf16[64,12,2048]{2,1,0:T(8,128)(2,1)}) %all-gather.3.cloned.1.call-update) | async-done | bytes 3145744 | tf_op jit(solution)/shard_map/all_gather | solution.py:40
  736.4 6.2 reshape.38
  742.6 3.9 convolution_convert_fusion
  746.5 4.8 multiply_reduce_fusion
  751.3 53.0 %psum.23 = bf16[256]{0:T(256)(128)(2,1)S(1)} all-reduce(bf16[256]{0:T(256)(128)(2,1)S(1)} %get-tuple-element.14), channel_id=1, replica_groups=mesh['layer'=4,'feat'=64] {'layer'}, use_global_device_ids=true, to_apply=%region_4.0 | all-reduce | flops 256 | bytes 1024 | tf_op jit(solution)/shard_map/psum | solution.py:55
  804.4 0.0 all-reduce.7.cloned.1.call-update
  804.4 1.8 multiply_bitcast_fusion
  806.2 3.5 copy.16
  809.7 40.2 %all-reduce.7.cloned.1.call-done = bf16[768,256]{1,0:T(8,128)(2,1)} async-done(((bf16[768,256]{1,0:T(8,128)(2,1)}), bf16[768,256]{1,0:T(8,128)(2,1)}) %all-reduce.7.cloned.1.call-update) | async-done | bytes 393232 | tf_op jit(solution)/shard_map/psum | solution.py:54
  849.9 4.0 fusion.4
  853.9 2.9 copy.15
  (43 shorter events, 0.1 us)
Async XLA Ops:
  7.2 165.3 %all-reduce.5.cloned.1.call-start = ((), (), s32[]{:S(2)}) async-start(), calls=%async_computation.1 | async-start | bytes 1572864 | tf_op jit(solution)/shard_map/psum | solution.py:29
  119.6 3.2 copy-start.13
  122.7 613.7 %all-gather.3.cloned.1.call-start = ((), (), s32[]{:S(2)}) async-start(), calls=%async_computation.3 | async-start | bytes 4259840 | tf_op jit(solution)/shard_map/all_gather | solution.py:40
  177.6 224.8 %copy-start.11 = (bf16[1,2048]{1,0:T(2,128)(2,1)S(1)}, bf16[1,2048]{1,0:T(2,128)(2,1)}, u32[]{:S(2)}) copy-start(bf16[1,2048]{1,0:T(2,128)(2,1)} %param.9) | copy-start | bytes 12292
  177.6 224.8 %copy-start.12 = (u32[256]{0:T(256)S(1)}, u32[256]{0:T(256)}, u32[]{:S(2)}) copy-start(u32[256]{0:T(256)} %constant.26) | copy-start | bytes 3076
  340.8 99.7 %copy-start = (bf16[12,1,2048]{2,0,1:T(8,128)(2,1)S(1)}, bf16[12,1,2048]{2,0,1:T(8,128)(2,1)}, u32[]{:S(2)}) copy-start(bf16[12,1,2048]{2,0,1:T(8,128)(2,1)} %param.5) | copy-start | bytes 147460
  340.9 13.7 %collective-permute-start.15 = (f32[12,2048]{1,0:T(8,128)S(1)}, f32[12,2048]{1,0:T(8,128)S(1)}, u32[]{:S(2)}, u32[]{:S(2)}) collective-permute-start(f32[12,2048]{1,0:T(8,128)S(1)} %slice), channel_id=1, source_target_pairs={{0,16},{1,17},{2,18},{3,19},{4,20},{5,21},{6,22},{7,23},{8,24},{9,... | collective-permute-start | bytes 294920
  342.2 19.5 %collective-permute-start = (f32[16,2048]{1,0:T(8,128)S(1)}, f32[16,2048]{1,0:T(8,128)S(1)}, u32[]{:S(2)}, u32[]{:S(2)}) collective-permute-start(f32[16,2048]{1,0:T(8,128)S(1)} %fusion), channel_id=1, source_target_pairs={{0,1},{1,2},{2,3},{3,4},{4,5},{5,6},{6,7},{7,8},{8,9},{9,10},{10,1... | collective-permute-start | bytes 393224
  343.5 19.8 %collective-permute-start.1 = (f32[16,2048]{1,0:T(8,128)S(1)}, f32[16,2048]{1,0:T(8,128)S(1)}, u32[]{:S(2)}, u32[]{:S(2)}) collective-permute-start(f32[16,2048]{1,0:T(8,128)S(1)} %fusion), channel_id=1, source_target_pairs={{0,2},{1,3},{2,4},{3,5},{4,6},{5,7},{6,8},{7,9},{8,10},{9,11},{10,... | collective-permute-start | bytes 393224
  344.8 22.9 %collective-permute-start.10 = (f32[16,2048]{1,0:T(8,128)S(1)}, f32[16,2048]{1,0:T(8,128)S(1)}, u32[]{:S(2)}, u32[]{:S(2)}) collective-permute-start(f32[16,2048]{1,0:T(8,128)S(1)} %fusion), channel_id=1, source_target_pairs={{0,11},{1,12},{2,13},{3,14},{4,15},{5,16},{6,17},{7,18},{8,19},{9,... | collective-permute-start | bytes 393224
  350.6 23.3 %collective-permute-start.11 = (f32[16,2048]{1,0:T(8,128)S(1)}, f32[16,2048]{1,0:T(8,128)S(1)}, u32[]{:S(2)}, u32[]{:S(2)}) collective-permute-start(f32[16,2048]{1,0:T(8,128)S(1)} %fusion), channel_id=1, source_target_pairs={{0,12},{1,13},{2,14},{3,15},{4,16},{5,17},{6,18},{7,19},{8,20},{9,... | collective-permute-start | bytes 393224
  354.6 20.6 %collective-permute-start.12 = (f32[16,2048]{1,0:T(8,128)S(1)}, f32[16,2048]{1,0:T(8,128)S(1)}, u32[]{:S(2)}, u32[]{:S(2)}) collective-permute-start(f32[16,2048]{1,0:T(8,128)S(1)} %fusion), channel_id=1, source_target_pairs={{0,13},{1,14},{2,15},{3,16},{4,17},{5,18},{6,19},{7,20},{8,21},{9,... | collective-permute-start | bytes 393224
  361.7 38.7 %copy-start.1 = (f32[16,2048]{1,0:T(8,128)}, f32[16,2048]{1,0:T(8,128)S(1)}, u32[]{:S(2)}) copy-start(f32[16,2048]{1,0:T(8,128)S(1)} %collective-permute-done) | copy-start | bytes 393220
  361.7 16.5 %collective-permute-start.13 = (f32[16,2048]{1,0:T(8,128)S(1)}, f32[16,2048]{1,0:T(8,128)S(1)}, u32[]{:S(2)}, u32[]{:S(2)}) collective-permute-start(f32[16,2048]{1,0:T(8,128)S(1)} %fusion), channel_id=1, source_target_pairs={{0,14},{1,15},{2,16},{3,17},{4,18},{5,19},{6,20},{7,21},{8,22},{9,... | collective-permute-start | bytes 393224
  363.3 38.9 %copy-start.2 = (f32[16,2048]{1,0:T(8,128)}, f32[16,2048]{1,0:T(8,128)S(1)}, u32[]{:S(2)}) copy-start(f32[16,2048]{1,0:T(8,128)S(1)} %collective-permute-done.1) | copy-start | bytes 393220
  363.3 19.4 %collective-permute-start.14 = (f32[16,2048]{1,0:T(8,128)S(1)}, f32[16,2048]{1,0:T(8,128)S(1)}, u32[]{:S(2)}, u32[]{:S(2)}) collective-permute-start(f32[16,2048]{1,0:T(8,128)S(1)} %fusion), channel_id=1, source_target_pairs={{0,15},{1,16},{2,17},{3,18},{4,19},{5,20},{6,21},{7,22},{8,23},{9,... | collective-permute-start | bytes 393224
  367.7 34.6 %copy-start.3 = (f32[16,2048]{1,0:T(8,128)}, f32[16,2048]{1,0:T(8,128)S(1)}, u32[]{:S(2)}) copy-start(f32[16,2048]{1,0:T(8,128)S(1)} %collective-permute-done.10) | copy-start | bytes 393220
  367.7 23.5 %collective-permute-start.2 = (f32[16,2048]{1,0:T(8,128)S(1)}, f32[16,2048]{1,0:T(8,128)S(1)}, u32[]{:S(2)}, u32[]{:S(2)}) collective-permute-start(f32[16,2048]{1,0:T(8,128)S(1)} %fusion), channel_id=1, source_target_pairs={{0,3},{1,4},{2,5},{3,6},{4,7},{5,8},{6,9},{7,10},{8,11},{9,12},{10... | collective-permute-start | bytes 393224
  373.8 28.4 %copy-start.4 = (f32[16,2048]{1,0:T(8,128)}, f32[16,2048]{1,0:T(8,128)S(1)}, u32[]{:S(2)}) copy-start(f32[16,2048]{1,0:T(8,128)S(1)} %collective-permute-done.11) | copy-start | bytes 393220
  373.9 20.3 %collective-permute-start.3 = (f32[16,2048]{1,0:T(8,128)S(1)}, f32[16,2048]{1,0:T(8,128)S(1)}, u32[]{:S(2)}, u32[]{:S(2)}) collective-permute-start(f32[16,2048]{1,0:T(8,128)S(1)} %fusion), channel_id=1, source_target_pairs={{0,4},{1,5},{2,6},{3,7},{4,8},{5,9},{6,10},{7,11},{8,12},{9,13},{1... | collective-permute-start | bytes 393224
  375.2 27.1 %copy-start.5 = (f32[16,2048]{1,0:T(8,128)}, f32[16,2048]{1,0:T(8,128)S(1)}, u32[]{:S(2)}) copy-start(f32[16,2048]{1,0:T(8,128)S(1)} %collective-permute-done.12) | copy-start | bytes 393220
  375.2 25.1 %collective-permute-start.4 = (f32[16,2048]{1,0:T(8,128)S(1)}, f32[16,2048]{1,0:T(8,128)S(1)}, u32[]{:S(2)}, u32[]{:S(2)}) collective-permute-start(f32[16,2048]{1,0:T(8,128)S(1)} %fusion), channel_id=1, source_target_pairs={{0,5},{1,6},{2,7},{3,8},{4,9},{5,10},{6,11},{7,12},{8,13},{9,14},{... | collective-permute-start | bytes 393224
  378.2 24.1 %copy-start.6 = (f32[16,2048]{1,0:T(8,128)}, f32[16,2048]{1,0:T(8,128)S(1)}, u32[]{:S(2)}) copy-start(f32[16,2048]{1,0:T(8,128)S(1)} %collective-permute-done.13) | copy-start | bytes 393220
  378.2 25.4 %collective-permute-start.5 = (f32[16,2048]{1,0:T(8,128)S(1)}, f32[16,2048]{1,0:T(8,128)}, u32[]{:S(2)}, u32[]{:S(2)}) collective-permute-start(f32[16,2048]{1,0:T(8,128)S(1)} %fusion), channel_id=1, source_target_pairs={{0,6},{1,7},{2,8},{3,9},{4,10},{5,11},{6,12},{7,13},{8,14},{9,15},... | collective-permute-start | bytes 393224
  382.8 19.5 %copy-start.7 = (f32[16,2048]{1,0:T(8,128)}, f32[16,2048]{1,0:T(8,128)S(1)}, u32[]{:S(2)}) copy-start(f32[16,2048]{1,0:T(8,128)S(1)} %collective-permute-done.14) | copy-start | bytes 393220
  382.8 20.9 %collective-permute-start.6 = (f32[16,2048]{1,0:T(8,128)S(1)}, f32[16,2048]{1,0:T(8,128)}, u32[]{:S(2)}, u32[]{:S(2)}) collective-permute-start(f32[16,2048]{1,0:T(8,128)S(1)} %fusion), channel_id=1, source_target_pairs={{0,7},{1,8},{2,9},{3,10},{4,11},{5,12},{6,13},{7,14},{8,15},{9,16}... | collective-permute-start | bytes 393224
  391.1 11.1 %copy-start.8 = (f32[16,2048]{1,0:T(8,128)}, f32[16,2048]{1,0:T(8,128)S(1)}, u32[]{:S(2)}) copy-start(f32[16,2048]{1,0:T(8,128)S(1)} %collective-permute-done.2) | copy-start | bytes 393220
  391.1 12.5 %collective-permute-start.7 = (f32[16,2048]{1,0:T(8,128)S(1)}, f32[16,2048]{1,0:T(8,128)}, u32[]{:S(2)}, u32[]{:S(2)}) collective-permute-start(f32[16,2048]{1,0:T(8,128)S(1)} %fusion), channel_id=1, source_target_pairs={{0,8},{1,9},{2,10},{3,11},{4,12},{5,13},{6,14},{7,15},{8,16},{9,17... | collective-permute-start | bytes 393224
  394.1 8.2 copy-start.9
  394.1 12.0 %collective-permute-start.8 = (f32[16,2048]{1,0:T(8,128)S(1)}, f32[16,2048]{1,0:T(8,128)}, u32[]{:S(2)}, u32[]{:S(2)}) collective-permute-start(f32[16,2048]{1,0:T(8,128)S(1)} %fusion), channel_id=1, source_target_pairs={{0,9},{1,10},{2,11},{3,12},{4,13},{5,14},{6,15},{7,16},{8,17},{9,1... | collective-permute-start | bytes 393224
  400.3 2.0 copy-start.10
  400.3 12.8 %collective-permute-start.9 = (f32[16,2048]{1,0:T(8,128)S(1)}, f32[16,2048]{1,0:T(8,128)}, u32[]{:S(2)}, u32[]{:S(2)}) collective-permute-start(f32[16,2048]{1,0:T(8,128)S(1)} %fusion), channel_id=1, source_target_pairs={{0,10},{1,11},{2,12},{3,13},{4,14},{5,15},{6,16},{7,17},{8,18},{9,... | collective-permute-start | bytes 393224
  442.2 407.7 %all-reduce.7.cloned.1.call-start = ((), (), s32[]{:S(2)}) async-start(), calls=%async_computation.2 | async-start | bytes 786432 | tf_op jit(solution)/shard_map/psum | solution.py:54
Sparse Core Ops, SparseCore 0:
  122.8 49.5 all-reduce.4
  442.4 294.0 all-gather.2
  804.5 45.3 all-reduce.6
